TPU v7x, 128 devices: a whole 4x4x4 slice. The times are simulated.
128 devices in a mesh: tm: 8 (over x, core), member: 16 (over z, y).
Axes of the slice: x: 4, y: 4, z: 4, core: 2. Of those that a mesh axis runs over, the one named last changes fastest.
Arguments:
- sensors: bfloat16 [16, 2048, 256], P('member', 'tm'), may hold values from -6 to 6
- kernel: bfloat16 [256, 256, 512], P('member'), may hold values from -0.0234375 to 0.0234375
- target: bfloat16 [16, 2048, 512], P('member', 'tm'), may hold values from -15 to 15
Outputs:
- errors: bfloat16 [16, 2048, 512], P('member', 'tm')
- whiteness: float32 [64, 512], replicated
All inputs are finite; a program needn't handle non-finite values.
Results may differ from a plain program's by a relative error of at most 0.0018.
Values may be sent and summed in bfloat16 or wider, within the bound.
No kernel may reach another device: no remote copies, remote signals or barrier semaphores. Data moves between devices by JAX's collectives and lax.ppermute only.
A program may use at most 64 MiB of HBM per device.

v0:
```python
import math
import jax
import jax.numpy as jnp
from jax import lax
from jax.sharding import PartitionSpec as P

LAGS = 64
EPS = 1e-06


def from_behind(shard, axis, by):
    peers = lax.axis_size(axis)
    pairs = [(i, i + by) for i in range(peers) if 0 <= i + by < peers]
    return lax.ppermute(shard, axis, pairs)


def shards(sensors, kernel, target):
    members_dev, steps_dev, channels = sensors.shape
    lag_dev = kernel.shape[0]
    kernel_span = lag_dev * lax.axis_size("member")
    first_lag = lax.axis_index("member") * lag_dev
    sensor_rim = from_behind(sensors, "tm", 1)
    joined = jnp.concatenate([sensor_rim, sensors], axis=1)
    gathered = lax.all_gather(joined, "member", axis=0, tiled=True)
    base = kernel_span - first_lag - (lag_dev - 1)

    def member_term(member_signal):
        block = lax.dynamic_slice_in_dim(member_signal, base, steps_dev + lag_dev - 1, 0)
        running = jnp.zeros((steps_dev, kernel.shape[2]), jnp.float32)
        for inner in range(lag_dev):
            window = block[lag_dev - 1 - inner : lag_dev - 1 - inner + steps_dev]
            running = running + jnp.dot(window, kernel[inner], preferred_element_type=jnp.float32)
        return running

    estimate = lax.psum_scatter(
        lax.map(member_term, gathered), "member", scatter_dimension=0, tiled=True
    )
    error_field = target.astype(jnp.float32) - estimate
    errors = error_field.astype(jnp.bfloat16)
    error_prior = from_behind(
        error_field[:, steps_dev - LAGS :, :].astype(jnp.bfloat16), "tm", 1
    ).astype(jnp.float32)
    joined_error = jnp.concatenate([error_prior, error_field], axis=1)

    def lag_sum(lag_index):
        window = lax.dynamic_slice_in_dim(joined_error, LAGS - lag_index, steps_dev, 1)
        return jnp.sum(error_field * window, axis=(0, 1))

    lag_partial = lax.map(lag_sum, jnp.arange(LAGS + 1, dtype=jnp.int32))
    totals = lax.psum(lag_partial, ("tm", "member"))
    sample_count = float(members_dev * lax.axis_size("member") * steps_dev * lax.axis_size("tm"))
    whiteness = (
        math.sqrt(sample_count) * (totals[1:] / sample_count) / (totals[0] / sample_count + EPS)
    )
    return (errors, whiteness)


def solution(mesh):
    in_specs = (P("member", "tm", None), P("member", None, None), P("member", "tm", None))
    out_specs = (P("member", "tm", None), P())
    return jax.shard_map(shards, mesh=mesh, in_specs=in_specs, out_specs=out_specs, check_vma=False)
```

profile of v0, /device:TPU:1, one launch (start us, length us, event | category | flops | bytes accessed | tf_op | source)
XLA Modules:
  0.0 877.6 jit_solution(1692239495963471276)
XLA Ops:
  7.2 4.5 collective-permute-start
  11.7 2.2 collective-permute-done
  15.7 54.4 %all-gather.2.cloned.1.call-done = bf16[16,512,256]{2,1,0:T(8,128)(2,1)} async-done(((bf16[1,512,256]{2,1,0:T(8,128)(2,1)}), bf16[16,512,256]{2,1,0:T(8,128)(2,1)}) %all-gather.2.cloned.1.call-update) | async-done | bytes 4194320 | tf_op jit(solution)/shard_map/all_gather | solution.py:24
  70.1 339.0 %while.25 = (s32[]{:T(128)}, f32[16,256,512]{2,1,0:T(8,128)}, bf16[16,512,256]{2,1,0:T(8,128)(2,1)}, s32[]{:T(128)}, bf16[16,256,512]{2,1,0:T(8,128)(2,1)}, /*in...) while((s32[]{:T(128)}, f32[16,256,512]{2,1,0:T(8,128)}, ...), condition=%wide.region_1.2_spmd, body=%wide.region_0.1_spmd.sunk | while | flops 1075707904 | bytes 22545932 | solution.py:36
  89.2 2.1 fusion.89
  110.3 2.1 fusion.89
  131.5 2.1 fusion.89
  152.7 2.1 fusion.89
  173.9 2.1 fusion.89
  195.1 2.1 fusion.89
  216.3 2.1 fusion.89
  237.4 2.1 fusion.89
  258.6 2.1 fusion.89
  279.8 2.1 fusion.89
  301.0 2.1 fusion.89
  322.2 2.1 fusion.89
  343.4 2.1 fusion.89
  364.6 2.1 fusion.89
  385.7 2.1 fusion.89
  406.9 2.1 fusion.89
  409.1 84.6 %reduce-scatter.4.cloned.1.call-done = f32[1,256,512]{2,1,0:T(8,128)} async-done(((f32[16,256,512]{2,1,0:T(8,128)}), f32[1,256,512]{2,1,0:T(8,128)}) %reduce-scatter.4.cloned.1.call-update) | async-done | bytes 524304
  494.9 5.1 collective-permute-start.1
  501.4 225.3 %while.26 = (s32[]{:T(128)}, f32[65,512]{1,0:T(8,128)}, s32[65]{0:T(128)S(1)}, f32[1,320,512]{2,1,0:T(8,128)S(1)}, f32[1,256,512]{2,1,0:T(8,128)S(1)}, /*index=5*/s32[]{:T(128)}, s32[1]{0:T(128)}, s32[]{:T(128)}, s32[1]{0:T(128)}) while((s32[]{:T(128)}, f32[65,512]{1,0:T(8,128)}, s32[65]{0:T(128)S(1)}, f32[1,320,512]{2,1,0:T(8,128)S(1)}, ...), condition=%wide.region_5.6_spmd, body=%wide.region_3.5_spmd.sunk | while | flops 261638 | bytes 1054879 | solution.py:49
  726.7 142.1 %all-reduce.3.cloned.1.call-done = f32[65,512]{1,0:T(8,128)} async-done(((f32[65,512]{1,0:T(8,128)}), f32[65,512]{1,0:T(8,128)}) %all-reduce.3.cloned.1.call-update) | async-done | bytes 133136 | tf_op jit(solution)/shard_map/psum | solution.py:50
  (456 shorter events, 445.9 us)
Async XLA Ops:
  7.2 62.9 %all-gather.2.cloned.1.call-start = ((), (), s32[]{:S(2)}) async-start(), calls=%async_computation.1 | async-start | bytes 4456448 | tf_op jit(solution)/shard_map/all_gather | solution.py:24
  7.2 6.7 collective-permute-start
  15.6 478.1 %reduce-scatter.4.cloned.1.call-start = ((), (), s32[]{:S(2)}) async-start(), calls=%async_computation.3 | async-start | bytes 8912896
  409.0 84.7 %copy-start.1 = (bf16[1,256,512]{2,1,0:T(8,128)(2,1)S(1)}, bf16[1,256,512]{2,1,0:T(8,128)(2,1)}, u32[]{:S(2)}) copy-start(bf16[1,256,512]{2,1,0:T(8,128)(2,1)} %param.9) | copy-start | bytes 786436
  409.0 459.7 %all-reduce.3.cloned.1.call-start = ((), (), s32[]{:S(2)}) async-start(), calls=%async_computation.2 | async-start | bytes 294912 | tf_op jit(solution)/shard_map/psum | solution.py:50
  494.8 376.2 %copy-start = (bf16[1,256,512]{2,1,0:T(8,128)(2,1)}, bf16[1,256,512]{2,1,0:T(8,128)(2,1)S(1)}, u32[]{:S(2)}) copy-start(bf16[1,256,512]{2,1,0:T(8,128)(2,1)S(1)} %get-tuple-element.186) | copy-start | bytes 786436
  494.9 6.4 collective-permute-start.1
Sparse Core Ops, SparseCore 0:
  15.7 54.2 all-gather.1
  409.2 84.5 reduce-scatter.3
  726.8 141.8 all-reduce.2
where the time goes:
time: 888 us; the launch traced here: 878 us
  matrix products  336 us (38%)
  waiting for transfers between devices  285 us (32%)
  local copies, waits for them, and re-layouts  129 us (15%)
  loops' own time  91.8 us (10%)
  between operations  13.8 us (2%)
  other arithmetic  12.2 us (1%)
  starting transfers between devices  9.73 us (1%)
    dot_general x256, matrix products, member_term(): jnp.dot(window, kernel[inner], preferred_element_type=jnp.float32)  336 us
    psum x1, waiting for transfers between devices, shards(): totals = lax.psum(lag_partial, ('tm', 'member'))  142 us
    another operation x1, loops' own time, shards(): lag_partial = lax.map(lag_sum, jnp.arange(LAGS + 1, dtype=jnp.int32))  89.2 us
    dynamic_update_slice x65, local copies, waits for them, and re-layouts, shards(): lag_partial = lax.map(lag_sum, jnp.arange(LAGS + 1, dtype=jnp.int32))  86.7 us
    unnamed x4, waiting for transfers between devices  84.7 us
    all_gather x1, waiting for transfers between devices, shards(): gathered = lax.all_gather(joined, 'member', axis=0, tiled=True)  54.4 us
    dynamic_slice x65, local copies, waits for them, and re-layouts, shards(): lag_partial = lax.map(lag_sum, jnp.arange(LAGS + 1, dtype=jnp.int32))  42.3 us
  transfers between devices with their start and end apart: 5, of which 5 were waited for; matrix products, arithmetic and copies ran while one was open for 0% of the time, Pallas kernels for 0%

commit v1 on v0

--- a/solution.py
+++ b/solution.py
@@ -47,7 +47,8 @@
         return jnp.sum(error_field * window, axis=(0, 1))
 
     lag_partial = lax.map(lag_sum, jnp.arange(LAGS + 1, dtype=jnp.int32))
-    totals = lax.psum(lag_partial, ("tm", "member"))
+    parts = lax.all_gather(lag_partial, ("tm", "member"), axis=0, tiled=False)
+    totals = parts.sum(axis=0)
     sample_count = float(members_dev * lax.axis_size("member") * steps_dev * lax.axis_size("tm"))
     whiteness = (
         math.sqrt(sample_count) * (totals[1:] / sample_count) / (totals[0] / sample_count + EPS)

time: 888 us -> 836 us (0.941)
  waiting for transfers between devices: 285 us -> 226 us
    psum x1 -> x0, waiting for transfers between devices: 142 us -> none  [shards(): totals = lax.psum(lag_partial, ('tm', 'member'))]
    all_gather x0 -> x1, waiting for transfers between devices: none -> 83.4 us  [shards(): parts = lax.all_gather(lag_partial, ('tm', 'member'), axis=0, tiled=False)]
where the time goes in v1:
time: 836 us; the launch traced here: 825 us
  matrix products  336 us (40%)
  waiting for transfers between devices  226 us (27%)
  local copies, waits for them, and re-layouts  129 us (15%)
  loops' own time  91.8 us (11%)
  other arithmetic  18.7 us (2%)
  between operations  13.8 us (2%)
  starting transfers between devices  9.73 us (1%)
    dot_general x256, matrix products, member_term(): jnp.dot(window, kernel[inner], preferred_element_type=jnp.float32)  336 us
    another operation x1, loops' own time, shards(): lag_partial = lax.map(lag_sum, jnp.arange(LAGS + 1, dtype=jnp.int32))  89.2 us
    dynamic_update_slice x65, local copies, waits for them, and re-layouts, shards(): lag_partial = lax.map(lag_sum, jnp.arange(LAGS + 1, dtype=jnp.int32))  86.7 us
    unnamed x4, waiting for transfers between devices  84.7 us
    all_gather x1, waiting for transfers between devices, shards(): parts = lax.all_gather(lag_partial, ('tm', 'member'), axis=0, tiled=False)  83.4 us
    all_gather x1, waiting for transfers between devices, shards(): gathered = lax.all_gather(joined, 'member', axis=0, tiled=True)  54.4 us
    dynamic_slice x65, local copies, waits for them, and re-layouts, shards(): lag_partial = lax.map(lag_sum, jnp.arange(LAGS + 1, dtype=jnp.int32))  42.3 us
  transfers between devices with their start and end apart: 5, of which 5 were waited for; matrix products, arithmetic and copies ran while one was open for 0% of the time, Pallas kernels for 0%

profile of v1, /device:TPU:1, one launch (start us, length us, event | category | flops | bytes accessed | tf_op | source)
XLA Modules:
  0.0 825.4 jit_solution(10836154203207526199)
XLA Ops:
  7.2 4.5 collective-permute-start
  11.7 2.2 collective-permute-done
  15.7 54.4 %all-gather.5.cloned.1.call-done = bf16[16,512,256]{2,1,0:T(8,128)(2,1)} async-done(((bf16[1,512,256]{2,1,0:T(8,128)(2,1)}), bf16[16,512,256]{2,1,0:T(8,128)(2,1)}) %all-gather.5.cloned.1.call-update) | async-done | bytes 4194320 | tf_op jit(solution)/shard_map/all_gather | solution.py:24
  70.1 339.0 %while.25 = (s32[]{:T(128)}, f32[16,256,512]{2,1,0:T(8,128)}, bf16[16,512,256]{2,1,0:T(8,128)(2,1)}, s32[]{:T(128)}, bf16[16,256,512]{2,1,0:T(8,128)(2,1)}, /*in...) while((s32[]{:T(128)}, f32[16,256,512]{2,1,0:T(8,128)}, ...), condition=%wide.region_1.2_spmd, body=%wide.region_0.1_spmd.sunk | while | flops 1075707904 | bytes 22545932 | solution.py:36
  89.2 2.1 fusion.89
  110.3 2.1 fusion.89
  131.5 2.1 fusion.89
  152.7 2.1 fusion.89
  173.9 2.1 fusion.89
  195.1 2.1 fusion.89
  216.3 2.1 fusion.89
  237.4 2.1 fusion.89
  258.6 2.1 fusion.89
  279.8 2.1 fusion.89
  301.0 2.1 fusion.89
  322.2 2.1 fusion.89
  343.4 2.1 fusion.89
  364.6 2.1 fusion.89
  406.9 2.1 fusion.89
  409.1 84.6 %reduce-scatter.4.cloned.1.call-done = f32[1,256,512]{2,1,0:T(8,128)} async-done(((f32[16,256,512]{2,1,0:T(8,128)}), f32[1,256,512]{2,1,0:T(8,128)}) %reduce-scatter.4.cloned.1.call-update) | async-done | bytes 524304
  494.9 5.1 collective-permute-start.1
  501.4 225.2 %while.26 = (s32[]{:T(128)}, f32[65,512]{1,0:T(8,128)}, s32[65]{0:T(128)S(1)}, f32[1,320,512]{2,1,0:T(8,128)S(1)}, f32[1,256,512]{2,1,0:T(8,128)S(1)}, /*index=5*/s32[]{:T(128)}, s32[1]{0:T(128)}, s32[]{:T(128)}, s32[1]{0:T(128)}) while((s32[]{:T(128)}, f32[65,512]{1,0:T(8,128)}, s32[65]{0:T(128)S(1)}, f32[1,320,512]{2,1,0:T(8,128)S(1)}, ...), condition=%wide.region_5.6_spmd, body=%wide.region_3.5_spmd.sunk | while | flops 261638 | bytes 1054879 | solution.py:49
  726.6 83.4 %all-gather.7.cloned.1.call-done = f32[128,65,512]{2,1,0:T(8,128)} async-done(((f32[1,65,512]{2,1,0:T(8,128)}), f32[128,65,512]{2,1,0:T(8,128)}) %all-gather.7.cloned.1.call-update) | async-done | bytes 17039376 | tf_op jit(solution)/shard_map/all_gather | solution.py:50
  810.1 8.1 reduce_sum.21
  (457 shorter events, 446.3 us)
Async XLA Ops:
  7.2 62.9 %all-gather.5.cloned.1.call-start = ((), (), s32[]{:S(2)}) async-start(), calls=%async_computation.1 | async-start | bytes 4456448 | tf_op jit(solution)/shard_map/all_gather | solution.py:24
  7.2 6.7 collective-permute-start
  15.6 478.1 %reduce-scatter.4.cloned.1.call-start = ((), (), s32[]{:S(2)}) async-start(), calls=%async_computation.3 | async-start | bytes 8912896
  409.0 84.7 %copy-start.1 = (bf16[1,256,512]{2,1,0:T(8,128)(2,1)S(1)}, bf16[1,256,512]{2,1,0:T(8,128)(2,1)}, u32[]{:S(2)}) copy-start(bf16[1,256,512]{2,1,0:T(8,128)(2,1)} %param.9) | copy-start | bytes 786436
  409.0 401.0 %all-gather.7.cloned.1.call-start = ((), (), s32[]{:S(2)}) async-start(), calls=%async_computation.2 | async-start | bytes 19021824 | tf_op jit(solution)/shard_map/all_gather | solution.py:50
  494.8 323.3 %copy-start = (bf16[1,256,512]{2,1,0:T(8,128)(2,1)}, bf16[1,256,512]{2,1,0:T(8,128)(2,1)S(1)}, u32[]{:S(2)}) copy-start(bf16[1,256,512]{2,1,0:T(8,128)(2,1)S(1)} %get-tuple-element.186) | copy-start | bytes 786436
  494.9 6.4 collective-permute-start.1
Sparse Core Ops, SparseCore 0:
  15.7 54.2 all-gather.4
  409.2 84.5 reduce-scatter.3
  726.8 83.2 all-gather.6
